TPU v7x, 256 devices: a whole 4x4x8 slice. The times are simulated.
256 devices in a mesh: shard: 32 (over x, z_hi, y), rep: 8 (over z_lo, core).
Axes of the slice: x: 4, y: 4, z: 8 (z_hi: 2, z_lo: 4; z = z_hi * 4 + z_lo), core: 2. Of those that a mesh axis runs over, the one named last changes fastest.
Arguments:
- momentum: bfloat16 [32, 512, 2048], P(None, 'shard'), may hold values from -6 to 6
- gradient: bfloat16 [32, 512, 2048], P(None, 'shard'), may hold values from -6 to 6
Outputs:
- new_momentum: bfloat16 [32, 512, 2048], P(None, 'shard')
- update: bfloat16 [32, 512, 2048], P(None, 'shard')
All inputs are finite; a program needn't handle non-finite values.
Results may differ from a plain program's by a relative error of at most 0.00065.
The roundings to bfloat16 on the way count: a program that leaves them out, or rounds other values in their place, can miss the bound.
Values may be sent and summed in bfloat16 or wider, within the bound.
A program may use at most 64 MiB of HBM per device.

v0:
```python
import jax
import jax.numpy as jnp
from jax import lax
from jax.sharding import PartitionSpec as P

ROWS = 512
COLS = 2048
ITERS = 5
coef_a = 3.4445
coef_b = -4.775
coef_c = 2.0315


def gram_sum(values):
    local_gram = jnp.dot(
        values, values.T, precision=lax.Precision.HIGHEST, preferred_element_type=jnp.float32
    )
    return lax.psum(local_gram, "rep")


def newton_step(gram_matrix, iterate):
    polynomial = coef_b * gram_matrix + coef_c * jnp.dot(
        gram_matrix, gram_matrix, precision=lax.Precision.HIGHEST
    )
    return coef_a * iterate + jnp.dot(polynomial, iterate, precision=lax.Precision.HIGHEST)


def shards(momentum, gradient):
    new_momentum = (0.95 * momentum.astype(jnp.float32) + gradient.astype(jnp.float32)).astype(
        jnp.bfloat16
    )
    blended = (gradient.astype(jnp.float32) + 0.95 * new_momentum.astype(jnp.float32)).astype(
        jnp.bfloat16
    )
    col_width = blended.shape[2] // lax.axis_size("rep")
    col_start = lax.axis_index("rep") * col_width
    col_block = lax.dynamic_slice_in_dim(blended, col_start, col_width, 2)
    regrouped = lax.all_to_all(col_block, "shard", split_axis=0, concat_axis=1, tiled=True)
    scale_value = jnp.sqrt(jnp.float32(max(ROWS, COLS)))
    columns_block = regrouped[0].astype(jnp.float32)
    square_total = lax.psum(jnp.sum(columns_block * columns_block), "rep")
    norm_value = jnp.sqrt(square_total) + 1e-07
    iterate = columns_block / norm_value
    gram_matrix = gram_sum(iterate)
    for sweep in range(ITERS):
        if sweep > 0:
            gram_matrix = gram_sum(iterate)
        iterate = newton_step(gram_matrix, iterate)
    result = (iterate * scale_value).astype(jnp.bfloat16)[None]
    full_matrix = lax.all_gather(result, "rep", axis=2, tiled=True)
    update = lax.all_to_all(full_matrix, "shard", split_axis=1, concat_axis=0, tiled=True)
    return (new_momentum, update)


def solution(mesh):
    return jax.shard_map(
        shards,
        mesh=mesh,
        in_specs=(P(None, "shard", None), P(None, "shard", None)),
        out_specs=(P(None, "shard", None), P(None, "shard", None)),
        check_vma=False,
    )
```

profile of v0, /device:TPU:1, one launch (start us, length us, event | category | flops | bytes accessed | tf_op | source)
XLA Modules:
  0.0 596.6 jit_solution(5018397277071204557)
XLA Ops:
  7.2 4.2 convert_element_type.28
  14.0 26.4 %all_to_all.21 = bf16[32,16,256]{2,1,0:T(8,128)(2,1)S(1)} all-to-all(bf16[32,16,256]{2,1,0:T(8,128)(2,1)S(1)} %fusion.8), channel_id=1, replica_groups=mesh['shard'=32,'rep'=8] {'shard'}, dimensions={0} | all-to-all | bytes 524288 | tf_op jit(solution)/shard_map/all_to_all | solution.py:38
  41.1 15.6 %psum.42 = f32[]{:T(128)} all-reduce(f32[]{:T(128)} %fusion.7), channel_id=1, replica_groups=mesh['shard'=32,'rep'=8] {'rep'}, use_global_device_ids=true, to_apply=%region_1.0 | all-reduce | flops 1 | bytes 8 | tf_op jit(solution)/shard_map/psum | solution.py:41
  57.5 2.0 fusion.9
  59.6 64.8 %all-reduce.6.cloned.1.call-done = f32[512,512]{1,0:T(8,128)} async-done(((f32[512,512]{1,0:T(8,128)}), f32[512,512]{1,0:T(8,128)}) %all-reduce.6.cloned.1.call-update) | async-done | bytes 1048592 | tf_op jit(solution)/shard_map/psum | solution.py:18
  124.4 3.9 fusion.4
  129.4 2.0 fusion.10
  131.4 73.5 %all-reduce.8.cloned.1.call-done = f32[512,512]{1,0:T(8,128)} async-done(((f32[512,512]{1,0:T(8,128)}), f32[512,512]{1,0:T(8,128)}) %all-reduce.8.cloned.1.call-update) | async-done | bytes 1048592 | tf_op jit(solution)/shard_map/psum | solution.py:18
  204.9 3.9 fusion.3
  212.1 73.3 %all-reduce.10.cloned.1.call-done = f32[512,512]{1,0:T(8,128)} async-done(((f32[512,512]{1,0:T(8,128)}), f32[512,512]{1,0:T(8,128)}) %all-reduce.10.cloned.1.call-update) | async-done | bytes 1048592 | tf_op jit(solution)/shard_map/psum | solution.py:18
  285.4 3.9 fusion.2
  290.3 2.0 fusion.12
  292.4 73.5 %all-reduce.12.cloned.1.call-done = f32[512,512]{1,0:T(8,128)} async-done(((f32[512,512]{1,0:T(8,128)}), f32[512,512]{1,0:T(8,128)}) %all-reduce.12.cloned.1.call-update) | async-done | bytes 1048592 | tf_op jit(solution)/shard_map/psum | solution.py:18
  365.9 3.9 fusion.1
  370.8 2.0 fusion.13
  373.1 73.2 %all-reduce.14.cloned.1.call-done = f32[512,512]{1,0:T(8,128)} async-done(((f32[512,512]{1,0:T(8,128)}), f32[512,512]{1,0:T(8,128)}) %all-reduce.14.cloned.1.call-update) | async-done | bytes 1048592 | tf_op jit(solution)/shard_map/psum | solution.py:18
  446.3 3.9 fusion
  452.0 40.6 %all-gather.3.cloned.1.call-done = bf16[512,2048]{1,0:T(8,128)(2,1)} async-done(((bf16[512,256]{1,0:T(8,128)(2,1)}), bf16[512,2048]{1,0:T(8,128)(2,1)}) %all-gather.3.cloned.1.call-update) | async-done | bytes 2097168 | tf_op jit(solution)/shard_map/all_gather | solution.py:50
  492.6 6.7 %copy.8 = bf16[1,512,2048]{2,0,1:T(2,128)(2,1)} copy(bf16[1,512,2048]{2,1,0:T(8,128)(2,1)} %bitcast.41) | data formatting | bytes 4194304 | tf_op jit(solution)/shard_map/all_gather | solution.py:50
  499.9 13.2 %reduce.3 = bf16[512,2048]{1,0:T(8,128)(2,1)S(1)} reduce(bf16[512,1,2048]{2,1,0:T(2,128)(2,1)} %bitcast.37, bf16[]{:T(256)} %broadcast.39), dimensions={1}, to_apply=%bitcast.36.reduce_sub_computation | reduce | bytes 4194306
  513.0 2.8 reshape.22
  515.8 62.4 %all_to_all.22 = bf16[32,2,16384]{2,1,0:T(2,128)(2,1)S(1)} all-to-all(bf16[32,2,16384]{2,1,0:T(2,128)(2,1)} %reshape.22), channel_id=1, replica_groups=mesh['shard'=32,'rep'=8] {'shard'}, dimensions={0} | all-to-all | bytes 4194304 | tf_op jit(solution)/shard_map/all_to_all | solution.py:51
  578.2 6.8 %reshape.23 = bf16[512,1,2048]{2,1,0:T(2,128)(2,1)} reshape(bf16[32,2,16384]{2,1,0:T(2,128)(2,1)S(1)} %all_to_all.22) | data formatting | bytes 4194304
  585.0 4.8 copy.6
  (29 shorter events, 12.2 us)
Async XLA Ops:
  7.2 117.3 %all-reduce.6.cloned.1.call-start = ((), (), s32[]{:S(2)}) async-start(), calls=%async_computation.2 | async-start | bytes 2097152 | tf_op jit(solution)/shard_map/psum | solution.py:18
  7.2 4.2 copy-start
  7.2 4.2 copy-start.2
  12.4 45.0 %copy-start.1 = (bf16[32,16,2048]{2,1,0:T(8,128)(2,1)}, bf16[32,16,2048]{2,1,0:T(8,128)(2,1)S(1)}, u32[]{:S(2)}) copy-start(bf16[32,16,2048]{2,1,0:T(8,128)(2,1)S(1)} %add_convert_fusion) | copy-start | bytes 6291460
  59.5 145.3 %all-reduce.8.cloned.1.call-start = ((), (), s32[]{:S(2)}) async-start(), calls=%async_computation.3 | async-start | bytes 2097152 | tf_op jit(solution)/shard_map/psum | solution.py:18
  131.4 154.0 %all-reduce.10.cloned.1.call-start = ((), (), s32[]{:S(2)}) async-start(), calls=%async_computation.4 | async-start | bytes 2097152 | tf_op jit(solution)/shard_map/psum | solution.py:18
  211.8 154.0 %all-reduce.12.cloned.1.call-start = ((), (), s32[]{:S(2)}) async-start(), calls=%async_computation.5 | async-start | bytes 2097152 | tf_op jit(solution)/shard_map/psum | solution.py:18
  292.3 154.0 %all-reduce.14.cloned.1.call-start = ((), (), s32[]{:S(2)}) async-start(), calls=%async_computation.6 | async-start | bytes 2097152 | tf_op jit(solution)/shard_map/psum | solution.py:18
  372.8 119.8 %all-gather.3.cloned.1.call-start = ((), (), s32[]{:S(2)}) async-start(), calls=%async_computation.7 | async-start | bytes 2359296 | tf_op jit(solution)/shard_map/all_gather | solution.py:50
Sparse Core Ops, SparseCore 0:
  59.7 64.7 all-reduce.5
  131.5 73.3 all-reduce.7
  212.0 73.3 all-reduce.9
  292.4 73.3 all-reduce.11
  373.0 73.3 all-reduce.13
  452.1 40.4 all-gather.2
where the time goes:
time: 597 us
  waiting for transfers between devices  399 us (67%)
  blocking collectives  104 us (17%)
  matrix products  35.3 us (6%)
  local copies, waits for them, and re-layouts  21.6 us (4%)
  other arithmetic  20.7 us (3%)
  between operations  14.9 us (2%)
    psum x5, waiting for transfers between devices, gram_sum(): return lax.psum(local_gram, 'rep')  358 us
    all_to_all x1, blocking collectives, shards(): lax.all_to_all(full_matrix, 'shard', split_axis=1, concat_axis=0, tiled=T...  62.4 us
    all_gather x1, waiting for transfers between devices, shards(): full_matrix = lax.all_gather(result, 'rep', axis=2, tiled=True)  40.6 us
    all_to_all x1, blocking collectives, shards(): lax.all_to_all(col_block, 'shard', split_axis=0, concat_axis=1, tiled=True)  26.4 us
    dot_general x5, matrix products, newton_step(): jnp.dot(gram_matrix, gram_matrix, precision=lax.Precision.HIGHEST)  19.6 us
    psum x1, blocking collectives, shards(): square_total = lax.psum(jnp.sum(columns_block * columns_block), 'rep')  15.6 us
    unnamed x10, local copies, waits for them, and re-layouts  14.8 us
    unnamed x1, other arithmetic  13.2 us
  transfers between devices with their start and end apart: 6, of which 6 were waited for; matrix products, arithmetic and copies ran while one was open for 0% of the time, Pallas kernels for 0%

commit v1 on v0

--- a/solution.py
+++ b/solution.py
@@ -11,11 +11,17 @@
 coef_c = 2.0315
 
 
+def summed_here(shard, axis):
+    parts = lax.all_gather(shard, axis, axis=0, tiled=False)
+    total = parts.sum(axis=0)
+    return total
+
+
 def gram_sum(values):
     local_gram = jnp.dot(
         values, values.T, precision=lax.Precision.HIGHEST, preferred_element_type=jnp.float32
     )
-    return lax.psum(local_gram, "rep")
+    return summed_here(local_gram, "rep")
 
 
 def newton_step(gram_matrix, iterate):

time: 597 us -> 706 us (1.18)
  waiting for transfers between devices: 399 us -> 494 us
  other arithmetic: 20.7 us -> 43.9 us
  matrix products: 35.3 us -> 25.1 us
    all_gather x0 -> x5, waiting for transfers between devices: none -> 455 us  [summed_here(): parts = lax.all_gather(shard, axis, axis=0, tiled=False)]
    psum x5 -> x0, waiting for transfers between devices: 358 us -> none  [gram_sum(): return lax.psum(local_gram, 'rep')]
    reduce_sum x0 -> x5, other arithmetic: none -> 22.5 us  [summed_here(): total = parts.sum(axis=0)]
    dot_general x5, matrix products: 19.6 us -> 9.4 us  [newton_step(): jnp.dot(gram_matrix, gram_matrix, precision=lax.Precision.HIGHEST)]
    unnamed x10 -> x8, local copies, waits for them, and re-layouts: 14.8 us -> 14.8 us
where the time goes in v1:
time: 706 us; the launch traced here: 705 us
  waiting for transfers between devices  494 us (70%)
  blocking collectives  104 us (15%)
  other arithmetic  43.9 us (6%)
  matrix products  25.1 us (4%)
  local copies, waits for them, and re-layouts  21.6 us (3%)
  between operations  14.9 us (2%)
    all_gather x5, waiting for transfers between devices, summed_here(): parts = lax.all_gather(shard, axis, axis=0, tiled=False)  455 us
    all_to_all x1, blocking collectives, shards(): lax.all_to_all(full_matrix, 'shard', split_axis=1, concat_axis=0, tiled=T...  62.4 us
    all_gather x1, waiting for transfers between devices, shards(): full_matrix = lax.all_gather(result, 'rep', axis=2, tiled=True)  39.8 us
    all_to_all x1, blocking collectives, shards(): lax.all_to_all(col_block, 'shard', split_axis=0, concat_axis=1, tiled=True)  26.4 us
    reduce_sum x5, other arithmetic, summed_here(): total = parts.sum(axis=0)  22.5 us
    psum x1, blocking collectives, shards(): square_total = lax.psum(jnp.sum(columns_block * columns_block), 'rep')  15.6 us
    unnamed x8, local copies, waits for them, and re-layouts  14.8 us
  transfers between devices with their start and end apart: 6, of which 6 were waited for; matrix products, arithmetic and copies ran while one was open for 0% of the time, Pallas kernels for 0%

profile of v1, /device:TPU:1, one launch (start us, length us, event | category | flops | bytes accessed | tf_op | source)
XLA Modules:
  0.0 705.1 jit_solution(12453261164874953601)
XLA Ops:
  7.2 4.2 convert_element_type.28
  11.4 2.1 add_convert_fusion
  14.8 26.4 %all_to_all.21 = bf16[32,16,256]{2,1,0:T(8,128)(2,1)S(1)} all-to-all(bf16[32,16,256]{2,1,0:T(8,128)(2,1)S(1)} %fusion.8), channel_id=1, replica_groups=mesh['shard'=32,'rep'=8] {'shard'}, dimensions={0} | all-to-all | bytes 524288 | tf_op jit(solution)/shard_map/all_to_all | solution.py:44
  41.9 15.6 %psum.7 = f32[]{:T(128)} all-reduce(f32[]{:T(128)} %fusion.7), channel_id=1, replica_groups=mesh['shard'=32,'rep'=8] {'rep'}, use_global_device_ids=true, to_apply=%region_1.0 | all-reduce | flops 1 | bytes 8 | tf_op jit(solution)/shard_map/psum | solution.py:47
  58.3 2.0 fusion.9
  60.4 84.8 %all-gather.13.cloned.1.call-done = f32[4096,512]{1,0:T(8,128)} async-done(((f32[512,512]{1,0:T(8,128)}), f32[4096,512]{1,0:T(8,128)}) %all-gather.13.cloned.1.call-update) | async-done | bytes 8388624 | tf_op jit(solution)/shard_map/all_gather | solution.py:15
  145.1 4.5 reduce_sum.55
  154.8 92.4 %all-gather.15.cloned.1.call-done = f32[4096,512]{1,0:T(8,128)} async-done(((f32[512,512]{1,0:T(8,128)}), f32[4096,512]{1,0:T(8,128)}) %all-gather.15.cloned.1.call-update) | async-done | bytes 8388624 | tf_op jit(solution)/shard_map/all_gather | solution.py:15
  247.1 4.5 reduce_sum.56
  256.6 92.5 %all-gather.17.cloned.1.call-done = f32[4096,512]{1,0:T(8,128)} async-done(((f32[512,512]{1,0:T(8,128)}), f32[4096,512]{1,0:T(8,128)}) %all-gather.17.cloned.1.call-update) | async-done | bytes 8388624 | tf_op jit(solution)/shard_map/all_gather | solution.py:15
  349.2 4.5 reduce_sum.57
  356.5 2.0 fusion.12
  358.6 92.5 %all-gather.19.cloned.1.call-done = f32[4096,512]{1,0:T(8,128)} async-done(((f32[512,512]{1,0:T(8,128)}), f32[4096,512]{1,0:T(8,128)}) %all-gather.19.cloned.1.call-update) | async-done | bytes 8388624 | tf_op jit(solution)/shard_map/all_gather | solution.py:15
  451.2 4.5 reduce_sum.58
  458.5 2.0 fusion.13
  460.8 92.3 %all-gather.21.cloned.1.call-done = f32[4096,512]{1,0:T(8,128)} async-done(((f32[512,512]{1,0:T(8,128)}), f32[4096,512]{1,0:T(8,128)}) %all-gather.21.cloned.1.call-update) | async-done | bytes 8388624 | tf_op jit(solution)/shard_map/all_gather | solution.py:15
  553.2 4.5 reduce_sum.59
  561.3 39.8 %all-gather.23.cloned.1.call-done = bf16[512,2048]{1,0:T(8,128)(2,1)} async-done(((bf16[512,256]{1,0:T(8,128)(2,1)}), bf16[512,2048]{1,0:T(8,128)(2,1)}) %all-gather.23.cloned.1.call-update) | async-done | bytes 2097168 | tf_op jit(solution)/shard_map/all_gather | solution.py:56
  601.1 6.7 copy.8
  608.4 13.2 %reduce.3 = bf16[512,2048]{1,0:T(8,128)(2,1)S(1)} reduce(bf16[512,1,2048]{2,1,0:T(2,128)(2,1)} %bitcast.42, bf16[]{:T(256)} %broadcast.39), dimensions={1}, to_apply=%bitcast.41.reduce_sub_computation | reduce | bytes 4194306
  621.5 2.8 reshape.27
  624.3 62.4 %all_to_all.22 = bf16[32,2,16384]{2,1,0:T(2,128)(2,1)S(1)} all-to-all(bf16[32,2,16384]{2,1,0:T(2,128)(2,1)} %reshape.27), channel_id=1, replica_groups=mesh['shard'=32,'rep'=8] {'shard'}, dimensions={0} | all-to-all | bytes 4194304 | tf_op jit(solution)/shard_map/all_to_all | solution.py:57
  686.7 6.8 reshape.28
  693.5 4.8 copy.6
  (32 shorter events, 22.3 us)
Async XLA Ops:
  7.2 4.3 copy-start
  7.2 138.0 %all-gather.13.cloned.1.call-start = ((), (), s32[]{:S(2)}) async-start(), calls=%async_computation.2 | async-start | bytes 9437184 | tf_op jit(solution)/shard_map/all_gather | solution.py:15
  7.2 4.2 copy-start.1
  60.3 186.8 %all-gather.15.cloned.1.call-start = ((), (), s32[]{:S(2)}) async-start(), calls=%async_computation.3 | async-start | bytes 9437184 | tf_op jit(solution)/shard_map/all_gather | solution.py:15
  154.6 194.6 %all-gather.17.cloned.1.call-start = ((), (), s32[]{:S(2)}) async-start(), calls=%async_computation.4 | async-start | bytes 9437184 | tf_op jit(solution)/shard_map/all_gather | solution.py:15
  256.6 194.6 %all-gather.19.cloned.1.call-start = ((), (), s32[]{:S(2)}) async-start(), calls=%async_computation.5 | async-start | bytes 9437184 | tf_op jit(solution)/shard_map/all_gather | solution.py:15
  358.6 194.6 %all-gather.21.cloned.1.call-start = ((), (), s32[]{:S(2)}) async-start(), calls=%async_computation.6 | async-start | bytes 9437184 | tf_op jit(solution)/shard_map/all_gather | solution.py:15
  460.6 140.5 %all-gather.23.cloned.1.call-start = ((), (), s32[]{:S(2)}) async-start(), calls=%async_computation.7 | async-start | bytes 2359296 | tf_op jit(solution)/shard_map/all_gather | solution.py:56
Sparse Core Ops, SparseCore 0:
  60.5 84.6 all-gather.12
  154.7 92.4 all-gather.14
  256.7 92.4 all-gather.16
  358.7 92.4 all-gather.18
  460.7 92.4 all-gather.20
  561.4 39.6 all-gather.22

commit v2 on v0

--- a/solution.py
+++ b/solution.py
@@ -48,7 +48,9 @@
         iterate = newton_step(gram_matrix, iterate)
     result = (iterate * scale_value).astype(jnp.bfloat16)[None]
     full_matrix = lax.all_gather(result, "rep", axis=2, tiled=True)
-    update = lax.all_to_all(full_matrix, "shard", split_axis=1, concat_axis=0, tiled=True)
+    pieces = jnp.split(full_matrix, lax.axis_size("shard"), axis=1)
+    received = lax.all_to_all(jnp.stack(pieces), "shard", 0, 0)
+    update = jnp.concatenate(received, axis=0)
     return (new_momentum, update)
 
 

time: 597 us -> 578 us (0.968)
  other arithmetic: 20.7 us -> 7.52 us
  local copies, waits for them, and re-layouts: 21.6 us -> 15.1 us
    unnamed x1 -> x0, other arithmetic: 13.2 us -> none
    all_gather x1 -> x0, local copies, waits for them, and re-layouts: 6.75 us -> none  [shards(): full_matrix = lax.all_gather(result, 'rep', axis=2, tiled=True)]
    unnamed x10 -> x40, local copies, waits for them, and re-layouts: 14.8 us -> 15.1 us
where the time goes in v2:
time: 578 us; the launch traced here: 577 us
  waiting for transfers between devices  399 us (69%)
  blocking collectives  104 us (18%)
  matrix products  35.1 us (6%)
  local copies, waits for them, and re-layouts  15.1 us (3%)
  between operations  15.1 us (3%)
  other arithmetic  7.52 us (1%)
    psum x5, waiting for transfers between devices, gram_sum(): return lax.psum(local_gram, 'rep')  359 us
    all_to_all x1, blocking collectives, shards(): received = lax.all_to_all(jnp.stack(pieces), 'shard', 0, 0)  62.2 us
    all_gather x1, waiting for transfers between devices, shards(): full_matrix = lax.all_gather(result, 'rep', axis=2, tiled=True)  40.6 us
    all_to_all x1, blocking collectives, shards(): lax.all_to_all(col_block, 'shard', split_axis=0, concat_axis=1, tiled=True)  26.4 us
    dot_general x5, matrix products, newton_step(): jnp.dot(gram_matrix, gram_matrix, precision=lax.Precision.HIGHEST)  19.4 us
    psum x1, blocking collectives, shards(): square_total = lax.psum(jnp.sum(columns_block * columns_block), 'rep')  15.6 us
    unnamed x40, local copies, waits for them, and re-layouts  15.1 us
  transfers between devices with their start and end apart: 6, of which 6 were waited for; matrix products, arithmetic and copies ran while one was open for 0% of the time, Pallas kernels for 0%

profile of v2, /device:TPU:1, one launch (start us, length us, event | category | flops | bytes accessed | tf_op | source)
XLA Modules:
  0.0 576.7 jit_solution(12165367721038447219)
XLA Ops:
  7.2 4.2 convert_element_type.28
  12.4 1.6 fusion.8
  14.0 26.4 %all_to_all.14 = bf16[32,16,256]{2,1,0:T(8,128)(2,1)S(1)} all-to-all(bf16[32,16,256]{2,1,0:T(8,128)(2,1)S(1)} %fusion.8), channel_id=1, replica_groups=mesh['shard'=32,'rep'=8] {'shard'}, dimensions={0} | all-to-all | bytes 524288 | tf_op jit(solution)/shard_map/all_to_all | solution.py:38
  41.1 15.6 %psum.42 = f32[]{:T(128)} all-reduce(f32[]{:T(128)} %fusion.7), channel_id=1, replica_groups=mesh['shard'=32,'rep'=8] {'rep'}, use_global_device_ids=true, to_apply=%region_1.0 | all-reduce | flops 1 | bytes 8 | tf_op jit(solution)/shard_map/psum | solution.py:41
  57.5 2.0 fusion.9
  59.6 64.8 %all-reduce.6.cloned.1.call-done = f32[512,512]{1,0:T(8,128)} async-done(((f32[512,512]{1,0:T(8,128)}), f32[512,512]{1,0:T(8,128)}) %all-reduce.6.cloned.1.call-update) | async-done | bytes 1048592 | tf_op jit(solution)/shard_map/psum | solution.py:18
  124.4 3.9 fusion.4
  129.3 2.0 fusion.10
  131.4 73.5 %all-reduce.8.cloned.1.call-done = f32[512,512]{1,0:T(8,128)} async-done(((f32[512,512]{1,0:T(8,128)}), f32[512,512]{1,0:T(8,128)}) %all-reduce.8.cloned.1.call-update) | async-done | bytes 1048592 | tf_op jit(solution)/shard_map/psum | solution.py:18
  204.9 3.9 fusion.3
  209.8 2.0 fusion.11
  212.0 73.3 %all-reduce.10.cloned.1.call-done = f32[512,512]{1,0:T(8,128)} async-done(((f32[512,512]{1,0:T(8,128)}), f32[512,512]{1,0:T(8,128)}) %all-reduce.10.cloned.1.call-update) | async-done | bytes 1048592 | tf_op jit(solution)/shard_map/psum | solution.py:18
  285.4 3.9 fusion.2
  290.3 2.0 fusion.12
  292.4 73.5 %all-reduce.12.cloned.1.call-done = f32[512,512]{1,0:T(8,128)} async-done(((f32[512,512]{1,0:T(8,128)}), f32[512,512]{1,0:T(8,128)}) %all-reduce.12.cloned.1.call-update) | async-done | bytes 1048592 | tf_op jit(solution)/shard_map/psum | solution.py:18
  365.8 3.9 fusion.1
  370.7 2.0 fusion.13
  372.8 73.5 %all-reduce.14.cloned.1.call-done = f32[512,512]{1,0:T(8,128)} async-done(((f32[512,512]{1,0:T(8,128)}), f32[512,512]{1,0:T(8,128)}) %all-reduce.14.cloned.1.call-update) | async-done | bytes 1048592 | tf_op jit(solution)/shard_map/psum | solution.py:18
  446.2 3.9 fusion
  450.1 1.7 fusion.6
  451.9 40.6 %all-gather.3.cloned.1.call-done = bf16[512,2048]{1,0:T(8,128)(2,1)} async-done(((bf16[512,256]{1,0:T(8,128)(2,1)}), bf16[512,2048]{1,0:T(8,128)(2,1)}) %all-gather.3.cloned.1.call-update) | async-done | bytes 2097168 | tf_op jit(solution)/shard_map/all_gather | solution.py:50
  492.5 1.0 constant_dynamic-update-slice_fusion.31
  506.4 62.2 %all_to_all.15 = bf16[32,1,16,2048]{3,2,1,0:T(8,128)(2,1)S(1)} all-to-all(bf16[32,1,16,2048]{3,2,1,0:T(8,128)(2,1)S(1)} %constant_dynamic-update-slice_fusion), channel_id=1, replica_groups=mesh['shard'=32,'rep'=8] {'shard'}, dimensions={0} | all-to-all | bytes 4194304 | tf_op jit(solution)/shard_map/all_to_all | solution.py:52
  568.6 1.3 copy.41
  (58 shorter events, 19.0 us)
Async XLA Ops:
  7.2 117.3 %all-reduce.6.cloned.1.call-start = ((), (), s32[]{:S(2)}) async-start(), calls=%async_computation.2 | async-start | bytes 2097152 | tf_op jit(solution)/shard_map/psum | solution.py:18
  7.2 4.2 copy-start
  7.2 4.2 copy-start.2
  12.4 47.1 %copy-start.1 = (bf16[32,16,2048]{2,1,0:T(8,128)(2,1)}, bf16[32,16,2048]{2,1,0:T(8,128)(2,1)S(1)}, u32[]{:S(2)}) copy-start(bf16[32,16,2048]{2,1,0:T(8,128)(2,1)S(1)} %add_convert_fusion) | copy-start | bytes 6291460
  59.5 145.3 %all-reduce.8.cloned.1.call-start = ((), (), s32[]{:S(2)}) async-start(), calls=%async_computation.3 | async-start | bytes 2097152 | tf_op jit(solution)/shard_map/psum | solution.py:18
  131.4 154.0 %all-reduce.10.cloned.1.call-start = ((), (), s32[]{:S(2)}) async-start(), calls=%async_computation.4 | async-start | bytes 2097152 | tf_op jit(solution)/shard_map/psum | solution.py:18
  211.8 154.0 %all-reduce.12.cloned.1.call-start = ((), (), s32[]{:S(2)}) async-start(), calls=%async_computation.5 | async-start | bytes 2097152 | tf_op jit(solution)/shard_map/psum | solution.py:18
  292.3 153.9 %all-reduce.14.cloned.1.call-start = ((), (), s32[]{:S(2)}) async-start(), calls=%async_computation.6 | async-start | bytes 2097152 | tf_op jit(solution)/shard_map/psum | solution.py:18
  372.7 119.7 %all-gather.3.cloned.1.call-start = ((), (), s32[]{:S(2)}) async-start(), calls=%async_computation.7 | async-start | bytes 2359296 | tf_op jit(solution)/shard_map/all_gather | solution.py:50
  492.5 13.7 %copy-start.3 = (bf16[512,2048]{1,0:T(8,128)(2,1)S(1)}, bf16[512,2048]{1,0:T(8,128)(2,1)}, u32[]{:S(2)}) copy-start(bf16[512,2048]{1,0:T(8,128)(2,1)} %all-gather.3.cloned.1.call-done) | copy-start | bytes 6291460
Sparse Core Ops, SparseCore 0:
  59.7 64.7 all-reduce.5
  131.5 73.3 all-reduce.7
  211.9 73.3 all-reduce.9
  292.4 73.3 all-reduce.11
  372.9 73.3 all-reduce.13
  452.0 40.4 all-gather.2
